TPU v7x, 32 devices: a whole 2x2x4 slice. The times are simulated.
32 devices in a mesh: dp: 4 (over z), expert: 8 (over y, x, core).
Axes of the slice: x: 2, y: 2, z: 4, core: 2. Of those that a mesh axis runs over, the one named last changes fastest.
Arguments:
- tokens: bfloat16 [32768, 768], P(('dp', 'expert')), may hold values from -6 to 6
- lengths: int32 [32], P(('dp', 'expert')), may hold values from 128 to 1024, as said below
- expert_index: int32 [32768], P(('dp', 'expert')), may hold values from 0 to 7, as said below
- centroids: float32 [8, 768], replicated, may hold values from -0.15625 to 0.15625
- input_weight: bfloat16 [768, 2304], replicated, may hold values from -0.3125 to 0.3125
- output_weight: bfloat16 [768, 768], replicated, may hold values from -0.875 to 0.875
- first_gain: float32 [768], replicated, may hold values from 0.5 to 1.5
- first_shift: float32 [768], replicated, may hold values from -1 to 1
- second_gain: float32 [768], replicated, may hold values from 0.5 to 1.5
- second_shift: float32 [768], replicated, may hold values from -1 to 1
- up_weight: bfloat16 [8, 768, 3072], P('expert'), may hold values from -0.21875 to 0.21875
- down_weight: bfloat16 [8, 3072, 768], P('expert'), may hold values from -0.3125 to 0.3125
- cotangent: bfloat16 [32768, 768], P(('dp', 'expert')), may hold values from -6 to 6
Outputs:
- layer_output: bfloat16 [32768, 768], P(('dp', 'expert'))
- input_gradient: bfloat16 [32768, 768], P(('dp', 'expert'))
- input_weight_gradient: float32 [768, 2304], P('dp')
- output_weight_gradient: float32 [768, 768], P('dp')
- first_gain_gradient: float32 [768], P('dp')
- first_shift_gradient: float32 [768], P('dp')
- second_gain_gradient: float32 [768], P('dp')
- second_shift_gradient: float32 [768], P('dp')
- up_weight_gradient: float32 [8, 768, 3072], P('expert', 'dp')
- down_weight_gradient: float32 [8, 3072, 768], P('expert', 'dp')
Inputs may be any that keep to these rules, and one draw needn't show every extreme that they name: `lengths`: some sequence has exactly 1024 live positions. `expert_index`: in each aligned block of 1024 rows (the sequences of one device), at most 128 rows inside their sequence's length name any one expert, and one expert, the same in every block, is named by exactly 128 of them.
All inputs are finite; a program needn't handle non-finite values.
Results may differ from a plain program's by a relative error of at most 0.015.
Values may be sent and summed in bfloat16 or wider, within the bound.
No kernel may reach another device: no remote copies, remote signals or barrier semaphores. Data moves between devices by JAX's collectives and lax.ppermute only.
A program may use at most 256 MiB of HBM per device.

v0:
```python
import jax
import jax.numpy as jnp
from jax import lax
from jax.sharding import PartitionSpec as P

HEADS = 12
LEN = 1024
epsilon = 1e-05
excluded = -1e30


def layer_norm(values, norm_gain, norm_shift):
    average = jnp.mean(values, axis=-1, keepdims=True)
    centred = values - average
    variance = jnp.mean(centred * centred, axis=-1, keepdims=True)
    return centred * lax.rsqrt(variance + epsilon) * norm_gain + norm_shift


def exact_gelu(values):
    return jax.nn.gelu(values, approximate=False)


def masked_scores(query_block, key_rows, lengths, first_row, scale_factor):
    scores = (
        jnp.einsum("sqhd,skhd->shqk", query_block, key_rows, preferred_element_type=jnp.float32)
        * scale_factor
    )
    rows = first_row + jnp.arange(query_block.shape[1])
    columns = jnp.arange(key_rows.shape[1])
    causal = columns[None, :] <= rows[:, None]
    inside = columns[None, :] < lengths[:, None]
    allowed = causal[None, None, :, :] & inside[:, None, None, :]
    return jnp.where(allowed, scores, excluded)


def on_device(
    tokens,
    lengths,
    expert_index,
    centroids,
    input_weight,
    output_weight,
    first_gain,
    first_shift,
    second_gain,
    second_shift,
    up_weight,
    down_weight,
    cotangent,
):
    row_count = tokens.shape[0]
    width = tokens.shape[1]
    sequences = lengths.shape[0]
    experts = centroids.shape[0]
    capacity = row_count // experts
    head_size = width // HEADS
    block = min(512, LEN)
    scale_factor = head_size ** (-0.5)
    split_heads = (sequences, LEN, HEADS, head_size)
    positions = jnp.arange(row_count)
    present = positions % LEN < jnp.repeat(lengths, LEN)
    row_mask = present.astype(jnp.float32)[:, None]
    inputs_float = tokens.astype(jnp.float32)
    normed, first_back = jax.vjp(layer_norm, inputs_float, first_gain, first_shift)
    normed_low = normed.astype(jnp.bfloat16)
    projected = jnp.dot(normed_low, input_weight, preferred_element_type=jnp.float32)
    queries = projected[:, :width].astype(jnp.bfloat16).reshape(split_heads)
    keys = projected[:, width : 2 * width].astype(jnp.bfloat16).reshape(split_heads)
    values = projected[:, 2 * width :].astype(jnp.bfloat16).reshape(split_heads)
    mixed_blocks = []
    kept_top = []
    kept_total = []
    for first_row in range(0, LEN, block):
        upto = first_row + block
        scores = masked_scores(
            queries[:, first_row:upto], keys[:, :upto], lengths, first_row, scale_factor
        )
        top = jnp.max(scores, axis=-1, keepdims=True)
        weights = jnp.exp(scores - top)
        total = jnp.sum(weights, axis=-1, keepdims=True)
        probs_low = (weights / total).astype(jnp.bfloat16)
        mixed_blocks.append(
            jnp.einsum(
                "shqk,skhd->sqhd", probs_low, values[:, :upto], preferred_element_type=jnp.float32
            )
        )
        kept_top.append(top)
        kept_total.append(total)
    mixed_low = jnp.concatenate(mixed_blocks, axis=1).reshape(row_count, width).astype(jnp.bfloat16)
    branch = jnp.dot(mixed_low, output_weight, preferred_element_type=jnp.float32)
    residual = inputs_float + row_mask * branch
    hidden, second_back = jax.vjp(layer_norm, residual, second_gain, second_shift)
    hidden_low = hidden.astype(jnp.bfloat16)
    onehot = expert_index[:, None] == jnp.arange(experts)[None, :]
    picked = jnp.dot(
        onehot.astype(jnp.float32),
        centroids,
        precision=lax.Precision.HIGHEST,
        preferred_element_type=jnp.float32,
    )
    gate = jax.nn.sigmoid(jnp.sum(hidden * picked, axis=-1))
    routed = onehot & present[:, None]
    counts = jnp.cumsum(routed.astype(jnp.int32), axis=0)
    slot = jnp.sum(jnp.where(routed, counts - 1, 0), axis=1)
    target = jnp.where(present, expert_index * capacity + slot, experts * capacity)
    outgoing = (
        jnp.zeros((experts * capacity, width), jnp.bfloat16)
        .at[target]
        .set(hidden_low, mode="drop")
        .reshape(experts, capacity, width)
    )
    arrived = lax.all_to_all(outgoing, "expert", split_axis=0, concat_axis=0, tiled=True)
    count = arrived.shape[1]
    flat = arrived.reshape(-1, width)
    upper = jnp.dot(flat, up_weight[0], preferred_element_type=jnp.float32)
    expert_active = exact_gelu(upper).astype(jnp.bfloat16)
    produced = jnp.dot(expert_active, down_weight[0], preferred_element_type=jnp.float32).astype(
        jnp.bfloat16
    )
    returned = lax.all_to_all(
        produced.reshape(experts, count, width), "expert", split_axis=0, concat_axis=0, tiled=True
    )
    results = (returned, arrived)
    returned = results[0]
    arrived = results[1]
    expert_term = jnp.take(
        returned.reshape(experts * capacity, width), target, axis=0, mode="fill", fill_value=0
    ).astype(jnp.float32)
    scaled = row_mask * gate[:, None]
    layer_output = (residual + scaled * expert_term).astype(jnp.bfloat16)
    upstream = cotangent.astype(jnp.float32)
    produced_gradient = (scaled * upstream).astype(jnp.bfloat16)
    logit_gradient = row_mask[:, 0] * jnp.sum(upstream * expert_term, axis=-1) * gate * (1.0 - gate)
    gradient_outgoing = (
        jnp.zeros((experts * capacity, width), jnp.bfloat16)
        .at[target]
        .set(produced_gradient, mode="drop")
        .reshape(experts, capacity, width)
    )
    arrived_gradient = lax.all_to_all(
        gradient_outgoing, "expert", split_axis=0, concat_axis=0, tiled=True
    ).reshape(-1, width)
    arrived_rows = arrived.reshape(-1, width)
    upper = jnp.dot(arrived_rows, up_weight[0], preferred_element_type=jnp.float32)
    active_float, gelu_back = jax.vjp(exact_gelu, upper)
    active = active_float.astype(jnp.bfloat16)
    dp_count = lax.axis_size("dp")
    part = active
    down_weight_gradient = lax.psum_scatter(
        jnp.einsum("rf,rd->fd", part, arrived_gradient, preferred_element_type=jnp.float32).astype(
            jnp.bfloat16
        ),
        "dp",
        scatter_dimension=0,
        tiled=True,
    ).astype(jnp.float32)
    active_gradient = jnp.einsum(
        "rd,fd->rf", arrived_gradient, down_weight[0], preferred_element_type=jnp.float32
    )
    upper_gradient = gelu_back(active_gradient)[0].astype(jnp.bfloat16)
    part = arrived_rows
    up_weight_gradient = lax.psum_scatter(
        jnp.einsum("rd,rf->df", part, upper_gradient, preferred_element_type=jnp.float32).astype(
            jnp.bfloat16
        ),
        "dp",
        scatter_dimension=0,
        tiled=True,
    ).astype(jnp.float32)
    sent_back = jnp.einsum(
        "rf,df->rd", upper_gradient, up_weight[0], preferred_element_type=jnp.float32
    ).astype(jnp.bfloat16)
    hidden_back = lax.all_to_all(
        sent_back.reshape(experts, capacity, width),
        "expert",
        split_axis=0,
        concat_axis=0,
        tiled=True,
    )
    expert_hidden = jnp.take(
        hidden_back.reshape(experts * capacity, width), target, axis=0, mode="fill", fill_value=0
    ).astype(jnp.float32)
    hidden_gradient = expert_hidden + logit_gradient[:, None] * picked
    residual_part, second_gain_gradient, second_shift_gradient = second_back(hidden_gradient)
    residual_gradient = upstream + residual_part
    branch_gradient = (row_mask * residual_gradient).astype(jnp.bfloat16)
    output_weight_gradient = jnp.einsum(
        "rd,re->de", mixed_low, branch_gradient, preferred_element_type=jnp.float32
    )
    mixed_gradient = (
        jnp.einsum("re,de->rd", branch_gradient, output_weight, preferred_element_type=jnp.float32)
        .astype(jnp.bfloat16)
        .reshape(split_heads)
    )
    query_blocks = []
    key_gradient = jnp.zeros(split_heads, jnp.float32)
    value_gradient = jnp.zeros(split_heads, jnp.float32)
    for number, first_row in enumerate(range(0, LEN, block)):
        upto = first_row + block
        query_block = queries[:, first_row:upto]
        scores = masked_scores(query_block, keys[:, :upto], lengths, first_row, scale_factor)
        probs = jnp.exp(scores - kept_top[number]) / kept_total[number]
        probs_low = probs.astype(jnp.bfloat16)
        incoming = mixed_gradient[:, first_row:upto]
        prob_gradient = jnp.einsum(
            "sqhd,skhd->shqk", incoming, values[:, :upto], preferred_element_type=jnp.float32
        )
        inner = jnp.sum(probs * prob_gradient, axis=-1, keepdims=True)
        score_gradient = (probs * (prob_gradient - inner)).astype(jnp.bfloat16)
        query_blocks.append(
            jnp.einsum(
                "shqk,skhd->sqhd",
                score_gradient,
                keys[:, :upto],
                preferred_element_type=jnp.float32,
            )
            * scale_factor
        )
        key_gradient = key_gradient.at[:, :upto].add(
            jnp.einsum(
                "shqk,sqhd->skhd", score_gradient, query_block, preferred_element_type=jnp.float32
            )
            * scale_factor
        )
        value_gradient = value_gradient.at[:, :upto].add(
            jnp.einsum("shqk,sqhd->skhd", probs_low, incoming, preferred_element_type=jnp.float32)
        )
    query_gradient = jnp.concatenate(query_blocks, axis=1)
    projected_gradient = jnp.concatenate(
        [
            query_gradient.reshape(row_count, width),
            key_gradient.reshape(row_count, width),
            value_gradient.reshape(row_count, width),
        ],
        axis=1,
    ).astype(jnp.bfloat16)
    input_weight_gradient = jnp.einsum(
        "rd,re->de", normed_low, projected_gradient, preferred_element_type=jnp.float32
    )
    normed_gradient = jnp.einsum(
        "re,de->rd", projected_gradient, input_weight, preferred_element_type=jnp.float32
    )
    input_part, first_gain_gradient, first_shift_gradient = first_back(normed_gradient)
    input_gradient = (residual_gradient + input_part).astype(jnp.bfloat16)
    gain_columns = jnp.stack(
        [first_gain_gradient, first_shift_gradient, second_gain_gradient, second_shift_gradient],
        axis=1,
    )
    total_input, total_output, total_gains = lax.psum(
        (input_weight_gradient, output_weight_gradient, gain_columns), ("dp", "expert")
    )
    share = width // dp_count
    begin = lax.axis_index("dp") * share
    input_share = lax.dynamic_slice_in_dim(total_input, begin, share, 0)
    output_share = lax.dynamic_slice_in_dim(total_output, begin, share, 0)
    gain_share = lax.dynamic_slice_in_dim(total_gains, begin, share, 0)
    return (
        layer_output,
        input_gradient,
        input_share,
        output_share,
        gain_share[:, 0],
        gain_share[:, 1],
        gain_share[:, 2],
        gain_share[:, 3],
        up_weight_gradient[None],
        down_weight_gradient[None],
    )


def solution(mesh):
    return jax.shard_map(
        on_device,
        mesh=mesh,
        in_specs=(
            P(("dp", "expert"), None),
            P(("dp", "expert")),
            P(("dp", "expert")),
            P(),
            P(),
            P(),
            P(),
            P(),
            P(),
            P(),
            P("expert", None, None),
            P("expert", None, None),
            P(("dp", "expert"), None),
        ),
        out_specs=(
            P(("dp", "expert"), None),
            P(("dp", "expert"), None),
            P("dp", None),
            P("dp", None),
            P("dp"),
            P("dp"),
            P("dp"),
            P("dp"),
            P("expert", "dp", None),
            P("expert", "dp", None),
        ),
        check_vma=False,
    )
```

profile of v0, /device:TPU:0, one launch (start us, length us, event | category | flops | bytes accessed | tf_op | source)
XLA Modules:
  0.0 812.4 jit_solution(16364089621944587762)
XLA Ops:
  43.2 13.4 %fusion.85 = f32[12,512,1024]{2,1,0:T(8,128)} fusion(bf16[1024,12,64]{0,2,1:T(8,128)(2,1)} %bitcast.177, bf16[1,1024,12,64]{1,3,2,0:T(8,128)(2,1)} %bitcast.181), kind=kOutput, calls=%fused_computation.133 | convolution fusion | flops 805306368 | bytes 27525120 | tf_op jit(solution)/shard_map/sqhd,skhd->shqk/dot_general | solution.py:25
  56.6 11.1 %fusion.121 = (f32[12,512]{1,0:T(8,128)}, f32[12,512,512]{1,2,0:T(8,128)}) fusion(pred[512,512]{0,1:T(8,128)(4,1)} %fusion.79, bf16[1,1024,12,64]{1,3,2,0:T(8,128)(2,1)} %bitcast.182, bf16[1,1024,12,64]{1,3,2,0:T(8,128)(2,1)} %bitcast.178), kind=kOutput, calls=%fused_computation.196 | convolution fusion | flops 415236608 | bytes 14442496 | tf_op jit(solution)/shard_map/sub | solution.py:79
  67.7 34.4 %fusion.120 = (f32[12,512]{1,0:T(8,128)}, f32[12,512,1024]{2,1,0:T(8,128)}) fusion(f32[12,512,1024]{2,1,0:T(8,128)} %fusion.85, pred[512,1024]{1,0:T(8,128)(4,1)} %fusion.49), kind=kOutput, calls=%fused_computation.195 | output fusion | flops 37749760 | bytes 50880512 | tf_op jit(solution)/shard_map/sub | solution.py:79
  108.1 10.3 %fusion.71 = bf16[1,512,12,64]{1,3,2,0:T(8,128)(2,1)S(1)} fusion(bf16[1024,12,64]{0,2,1:T(8,128)(2,1)S(1)} %bitcast.195, f32[12,512,1024]{2,1,0:T(8,128)} %get-tuple-element.121, f32[12,512]{1,0:T(8,128)S(1)} %copy-done.50), kind=kOutput, calls=%fused_computation.114 | convolution fusion | flops 818282496 | bytes 27549696 | tf_op jit(solution)/shard_map/shqk,skhd->sqhd/dot_general | solution.py:83
  139.2 26.6 %all_to_all.20 = bf16[8,128,768]{2,1,0:T(8,128)(2,1)S(1)} all-to-all(bf16[8,128,768]{2,1,0:T(8,128)(2,1)} %bitcast.188), channel_id=1, replica_groups=mesh['dp'=4,'expert'=8] {'expert'}, dimensions={0} | all-to-all | bytes 3145728 | tf_op jit(solution)/shard_map/all_to_all | solution.py:112
  165.8 35.7 %multiply_convert_fusion.2 = (bf16[1024,3072]{1,0:T(8,128)(2,1)S(1)}, f32[1024,3072]{1,0:T(8,128)}, f32[1024,3072]{1,0:T(8,128)}) fusion(bf16[1024,768]{1,0:T(8,128)(2,1)S(1)} %bitcast.191, bf16[1,768,3072]{2,1,0:T(8,128)(2,1)} %param.37), kind=kOutput, calls=%fused_computation.16 | convolution fusion | flops 5036310528 | bytes 37748736 | tf_op jit(solution)/shard_map/dot_general | solution.py:115
  201.5 10.7 %fusion.57 = bf16[1024,768]{1,0:T(8,128)(2,1)} fusion(bf16[1024,3072]{1,0:T(8,128)(2,1)S(1)} %get-tuple-element.106, bf16[1,3072,768]{2,1,0:T(8,128)(2,1)} %param.38), kind=kOutput, calls=%fused_computation.102 | convolution fusion | flops 4832624640 | bytes 12582912 | tf_op jit(solution)/shard_map/dot_general | solution.py:117
  219.2 18.4 %all-to-all-done.1 = bf16[8,128,768]{2,1,0:T(8,128)(2,1)} async-done(((bf16[8,128,768]{2,1,0:T(8,128)(2,1)}), bf16[8,128,768]{2,1,0:T(8,128)(2,1)}, u32[]{:S(2)}, u32[]{:S(2)}) %all-to-all-start.1) | async-done | bytes 1572896 | tf_op jit(solution)/shard_map/all_to_all | solution.py:120
  237.6 7.2 gather_fusion
  261.4 24.7 %all_to_all.21 = bf16[8,128,768]{2,1,0:T(8,128)(2,1)S(1)} all-to-all(bf16[8,128,768]{2,1,0:T(8,128)(2,1)} %bitcast.187), channel_id=1, replica_groups=mesh['dp'=4,'expert'=8] {'expert'}, dimensions={0} | all-to-all | bytes 3145728 | tf_op jit(solution)/shard_map/all_to_all | solution.py:140
  286.0 16.4 %add_convert_fusion = bf16[1024,3072]{1,0:T(8,128)(2,1)} fusion(f32[1024,3072]{1,0:T(8,128)} %get-tuple-element.107, f32[1024,3072]{1,0:T(8,128)} %get-tuple-element.127, bf16[1024,768]{1,0:T(8,128)(2,1)S(1)} %bitcast.199, bf16[1,3072,768]{2,1,0:T(8,128)(2,1)} %param.38), kind=kOutput, calls=%fused_computation.15 | convolution fusion | flops 4875878400 | bytes 37748736 | tf_op jit(solution)/shard_map/rd,fd->rf/dot_general | solution.py:157
  302.4 9.5 %fusion.54 = bf16[1024,768]{1,0:T(8,128)(2,1)} fusion(bf16[1024,3072]{1,0:T(8,128)(2,1)} %add_convert_fusion, bf16[1,768,3072]{2,1,0:T(8,128)(2,1)} %param.37), kind=kOutput, calls=%fused_computation.101 | convolution fusion | flops 4832624640 | bytes 12582912 | tf_op jit(solution)/shard_map/rf,df->rd/dot_general | solution.py:170
  316.4 21.0 %all-to-all-done.3 = bf16[8,128,768]{2,1,0:T(8,128)(2,1)} async-done(((bf16[8,128,768]{2,1,0:T(8,128)(2,1)}), bf16[8,128,768]{2,1,0:T(8,128)(2,1)}, u32[]{:S(2)}, u32[]{:S(2)}) %all-to-all-start.3) | async-done | bytes 1572896 | tf_op jit(solution)/shard_map/all_to_all | solution.py:173
  337.3 7.2 gather_fusion.1
  385.9 17.8 %multiply_reduce_fusion = (f32[12,512]{1,0:T(8,128)}, f32[12,512,1024]{2,1,0:T(8,128)}) fusion(f32[12,512,1024]{2,1,0:T(8,128)} %get-tuple-element.121, f32[12,512]{1,0:T(8,128)} %get-tuple-element.120, bf16[1024,12,64]{0,2,1:T(8,128)(2,1)} %bitcast.194, bf16[1,1024,12,64]{1,3,2,0:T(8,128)(2,1)} %bitcast.215), kind=kOutput, calls=%fused_computation.7 | convolution fusion | flops 824174592 | bytes 52748288 | tf_op jit(solution)/shard_map/sqhd,skhd->shqk/dot_general | solution.py:205
  403.7 10.6 %fusion.42 = bf16[1,1024,12,64]{1,3,2,0:T(8,128)(2,1)S(1)} fusion(f32[1,512,12,64]{1,3,2,0:T(8,128)} %fusion.60, bf16[1,1024,12,64]{1,3,2,0:T(8,128)(2,1)} %bitcast.216, f32[12,512,1024]{2,1,0:T(8,128)} %get-tuple-element.121, f32[12,512]{1,0:T(8,128)} %get-tuple-element.120), kind=kOutput, calls=%fused_computation.81 | convolution fusion | flops 819462144 | bytes 29130752 | tf_op jit(solution)/shard_map/shqk,sqhd->skhd/dot_general | solution.py:226
  414.4 21.8 %multiply_convert_fusion = bf16[12,512,1024]{2,1,0:T(8,128)(2,1)} fusion(f32[12,512,1024]{2,1,0:T(8,128)} %get-tuple-element.131, f32[12,512]{1,0:T(8,128)S(1)} %copy-done.52, f32[12,512,1024]{2,1,0:T(8,128)} %get-tuple-element.121, f32[12,512]{1,0:T(8,128)S(1)} %copy-done.51), kind=kLoop, calls=%fused_computation.6 | loop fusion | flops 25165824 | bytes 62963712 | tf_op jit(solution)/shard_map/convert_element_type | solution.py:209
  436.2 8.6 %fusion.77 = bf16[1,512,12,64]{1,3,2,0:T(8,128)(2,1)S(1)} fusion(bf16[1024,12,64]{0,2,1:T(8,128)(2,1)S(1)} %bitcast.180, bf16[12,512,1024]{2,1,0:T(8,128)(2,1)} %multiply_convert_fusion), kind=kOutput, calls=%fused_computation.116 | convolution fusion | flops 806092800 | bytes 14942208 | tf_op jit(solution)/shard_map/shqk,skhd->sqhd/dot_general | solution.py:211
  454.4 7.1 fusion.50
  461.5 9.1 %convolution_convert_fusion.1 = bf16[3072,768]{1,0:T(8,128)(2,1)} fusion(bf16[1024,3072]{1,0:T(8,128)(2,1)} %copy-done.72, bf16[1024,768]{1,0:T(8,128)(2,1)} %bitcast.200), kind=kOutput, calls=%fused_computation.46 | convolution fusion | flops 4834197504 | bytes 12582912 | tf_op jit(solution)/shard_map/rf,rd->fd/dot_general | solution.py:150
  470.8 9.5 %convolution_convert_fusion.2 = bf16[768,3072]{1,0:T(8,128)(2,1)} fusion(bf16[1024,768]{1,0:T(8,128)(2,1)} %bitcast.192, bf16[1024,3072]{1,0:T(8,128)(2,1)} %add_convert_fusion), kind=kOutput, calls=%fused_computation.47 | convolution fusion | flops 4834197504 | bytes 12582912 | tf_op jit(solution)/shard_map/rd,rf->df/dot_general | solution.py:163
  484.7 7.9 fusion.123
  508.8 43.2 %psum.23 = f32[768,4]{0,1:T(4,128)} all-reduce(f32[768,4]{0,1:T(4,128)S(1)} %pad_maximum_fusion.5), channel_id=1, replica_groups=mesh['dp'=4,'expert'=8] {'dp','expert'}, use_global_device_ids=true, to_apply=%region_27.29 | all-reduce | flops 3072 | bytes 24576 | tf_op jit(solution)/shard_map/psum | solution.py:249
  553.4 240.9 %all-reduce.5.cloned.1.call-done = (f32[768,2304]{1,0:T(8,128)}, f32[768,768]{1,0:T(8,128)}) async-done(((f32[768,2304]{1,0:T(8,128)}, f32[768,768]{1,0:T(8,128)}), (f32[768,2304]{1,0:T(8,128)}, f32[768,768]{1,0:T(8,128)})) %all-reduce.5.cloned.1.call-update) | async-done | bytes 9437200 | tf_op jit(solution)/shard_map/psum | solution.py:249
  (237 shorter events, 172.1 us)
Async XLA Ops:
  8.0 19.3 %copy-start = (bf16[768,2304]{1,0:T(8,128)(2,1)S(1)}, bf16[768,2304]{1,0:T(8,128)(2,1)}, u32[]{:S(2)}) copy-start(bf16[768,2304]{1,0:T(8,128)(2,1)} %param.31) | copy-start | bytes 10616836
  9.9 108.8 %copy-start.56 = (f32[1024]{0:T(1024)}, f32[1024]{0:T(1024)S(1)}, u32[]{:S(2)}) copy-start(f32[1024]{0:T(1024)S(1)} %fusion.106) | copy-start | bytes 12292
  20.4 6.9 copy-start.68
  24.9 6.9 copy-start.30
  132.2 69.3 %copy-start.58 = (s32[1024]{0:T(1024)}, s32[1024]{0:T(1024)S(1)}, u32[]{:S(2)}) copy-start(s32[1024]{0:T(1024)S(1)} %get-tuple-element.105) | copy-start | bytes 12292
  165.8 35.7 %copy-start.21 = (bf16[8,128,768]{2,1,0:T(8,128)(2,1)}, bf16[8,128,768]{2,1,0:T(8,128)(2,1)S(1)}, u32[]{:S(2)}) copy-start(bf16[8,128,768]{2,1,0:T(8,128)(2,1)S(1)} %all_to_all.20) | copy-start | bytes 4718596
  201.5 10.7 %copy-start.72 = (bf16[1024,3072]{1,0:T(8,128)(2,1)}, bf16[1024,3072]{1,0:T(8,128)(2,1)S(1)}, u32[]{:S(2)}) copy-start(bf16[1024,3072]{1,0:T(8,128)(2,1)S(1)} %get-tuple-element.106) | copy-start | bytes 18874372
  212.2 6.9 copy-start.59
  212.2 6.9 copy-start.45
  212.2 25.4 %all-to-all-start.1 = ((bf16[8,128,768]{2,1,0:T(8,128)(2,1)}), bf16[8,128,768]{2,1,0:T(8,128)(2,1)}, u32[]{:S(2)}, u32[]{:S(2)}) async-start(bf16[8,128,768]{2,1,0:T(8,128)(2,1)} %bitcast.204), calls=%async_computation.1 | async-start | bytes 3145728 | tf_op jit(solution)/shard_map/all_to_all | solution.py:120
  219.1 28.2 %copy-start.48 = (f32[1024]{0:T(1024)}, f32[1024]{0:T(1024)S(1)}, u32[]{:S(2)}) copy-start(f32[1024]{0:T(1024)S(1)} %broadcast_select_fusion.1) | copy-start | bytes 12292
  286.0 16.4 %copy-start.26 = (bf16[8,128,768]{2,1,0:T(8,128)(2,1)}, bf16[8,128,768]{2,1,0:T(8,128)(2,1)S(1)}, u32[]{:S(2)}) copy-start(bf16[8,128,768]{2,1,0:T(8,128)(2,1)S(1)} %all_to_all.21) | copy-start | bytes 4718596
  311.9 25.5 %all-to-all-start.3 = ((bf16[8,128,768]{2,1,0:T(8,128)(2,1)}), bf16[8,128,768]{2,1,0:T(8,128)(2,1)}, u32[]{:S(2)}, u32[]{:S(2)}) async-start(bf16[8,128,768]{2,1,0:T(8,128)(2,1)} %bitcast.203), calls=%async_computation.3 | async-start | bytes 3145728 | tf_op jit(solution)/shard_map/all_to_all | solution.py:173
  316.3 478.0 %all-reduce.5.cloned.1.call-start = ((), (), s32[]{:S(2)}) async-start(), calls=%async_computation.8 | async-start | bytes 18874368 | tf_op jit(solution)/shard_map/psum | solution.py:249
  373.8 6.9 copy-start.8
  403.7 10.6 %copy-start.51 = (f32[12,512]{1,0:T(8,128)S(1)}, f32[12,512]{1,0:T(8,128)}, u32[]{:S(2)}) copy-start(f32[12,512]{1,0:T(8,128)} %get-tuple-element.120) | copy-start | bytes 73732
  403.7 10.6 %copy-start.52 = (f32[12,512]{1,0:T(8,128)S(1)}, f32[12,512]{1,0:T(8,128)}, u32[]{:S(2)}) copy-start(f32[12,512]{1,0:T(8,128)} %get-tuple-element.130) | copy-start | bytes 73732
  414.3 37.8 %copy-start.70 = (bf16[1,1024,12,64]{1,3,2,0:T(8,128)(2,1)}, bf16[1,1024,12,64]{1,3,2,0:T(8,128)(2,1)S(1)}, u32[]{:S(2)}) copy-start(bf16[1,1024,12,64]{1,3,2,0:T(8,128)(2,1)S(1)} %fusion.42) | copy-start | bytes 4718596
  414.3 21.9 %copy-start.9 = (bf16[1024,768]{0,1:T(8,128)(2,1)S(1)}, bf16[1024,768]{0,1:T(8,128)(2,1)}, u32[]{:S(2)}) copy-start(bf16[1024,768]{0,1:T(8,128)(2,1)} %copy.46) | copy-start | bytes 4718596
  436.2 8.7 %copy-start.16 = (bf16[1024,768]{0,1:T(8,128)(2,1)S(1)}, bf16[1024,768]{0,1:T(8,128)(2,1)}, u32[]{:S(2)}) copy-start(bf16[1024,768]{0,1:T(8,128)(2,1)} %copy.45) | copy-start | bytes 4718596
  436.2 8.7 %copy-start.18 = (f32[1,512,12,64]{1,3,2,0:T(8,128)S(1)}, f32[1,512,12,64]{1,3,2,0:T(8,128)}, u32[]{:S(2)}) copy-start(f32[1,512,12,64]{1,3,2,0:T(8,128)} %multiply_bitcast_fusion) | copy-start | bytes 4718596
  444.9 7.0 copy-start.20
  461.5 337.5 %reduce-scatter.5.cloned.1.call-start = ((), (), s32[]{:S(2)}) async-start(), calls=%async_computation.7 | async-start | bytes 5898240 | tf_op jit(solution)/shard_map/reduce_scatter | solution.py:149
  470.7 331.2 %reduce-scatter.3.cloned.1.call-start = ((), (), s32[]{:S(2)}) async-start(), calls=%async_computation.6 | async-start | bytes 5898240 | tf_op jit(solution)/shard_map/reduce_scatter | solution.py:162
  (57 other events, 194.5 us)
Sparse Core Ops, SparseCore 0:
  461.6 332.6 all-reduce.4
Sparse Core Ops, SparseCore 1:
  470.8 99.6 reduce-scatter.4
  572.8 97.5 reduce-scatter.2
where the time goes:
time: 818 us; the launch traced here: 812 us
  waiting for transfers between devices  280 us (34%)
  matrix products  220 us (27%)
  other arithmetic  109 us (13%)
  blocking collectives  94.5 us (12%)
  local copies, waits for them, and re-layouts  82.5 us (10%)
  between operations  17.3 us (2%)
  starting transfers between devices  8.87 us (1%)
    psum x1, waiting for transfers between devices, on_device(): lax.psum((input_weight_gradient, output_weight_gradient, gain_columns), (...  241 us
    psum x1, blocking collectives, on_device(): lax.psum((input_weight_gradient, output_weight_gradient, gain_columns), (...  43.2 us
    dot_general x1, matrix products, on_device(): upper = jnp.dot(flat, up_weight[0], preferred_element_type=jnp.float32)  35.7 us
    sub x1, other arithmetic, on_device(): weights = jnp.exp(scores - top)  34.4 us
    convert_element_type x2, other arithmetic, on_device(): score_gradient = (probs * (prob_gradient - inner)).astype(jnp.bfloat16)  28.8 us
    all_to_all x1, blocking collectives, on_device(): lax.all_to_all(outgoing, 'expert', split_axis=0, concat_axis=0, tiled=True)  26.6 us
    all_to_all x1, blocking collectives, on_device(): lax.all_to_all(gradient_outgoing, 'expert', split_axis=0, concat_axis=0,...  24.7 us
    dot_general x2, matrix products, on_device(): jnp.einsum('sqhd,skhd->shqk', incoming, values[:, :upto], preferred_eleme...  23.5 us
  transfers between devices with their start and end apart: 5, of which 3 were waited for; matrix products, arithmetic and copies ran while one was open for 7% of the time, Pallas kernels for 0%

commit v1 on v0

--- a/solution.py
+++ b/solution.py
@@ -247,7 +247,7 @@
         axis=1,
     )
     total_input, total_output, total_gains = lax.psum(
-        (input_weight_gradient, output_weight_gradient, gain_columns), ("dp", "expert")
+        lax.psum((input_weight_gradient, output_weight_gradient, gain_columns), "expert"), "dp"
     )
     share = width // dp_count
     begin = lax.axis_index("dp") * share

time: 818 us -> 990 us (1.21)
  waiting for transfers between devices: 280 us -> 452 us
    psum x1 -> x2, waiting for transfers between devices: 241 us -> 413 us  [the longest x1 294 us: on_device(): lax.psum(lax.psum((input_weight_gradient, output_weight_gradient, gain_co...]
    psum x1 -> x2, blocking collectives: 43.2 us -> 44.2 us  [the longest x1 23.4 us: on_device(): lax.psum((input_weight_gradient, output_weight_gradient, gain_columns), '...]
  transfers between devices with their start and end apart: 5 -> 6, of which waited for: 3 -> 4; matrix products, arithmetic and copies ran while one was open for 7% -> 6% of each run, Pallas kernels for 0% -> 0%
where the time goes in v1:
time: 990 us; the launch traced here: 984 us
  waiting for transfers between devices  452 us (46%)
  matrix products  220 us (22%)
  other arithmetic  109 us (11%)
  blocking collectives  95.5 us (10%)
  local copies, waits for them, and re-layouts  81.5 us (8%)
  between operations  17.5 us (2%)
    psum x1, waiting for transfers between devices, on_device(): lax.psum(lax.psum((input_weight_gradient, output_weight_gradient, gain_co...  294 us
    psum x1, waiting for transfers between devices, on_device(): lax.psum((input_weight_gradient, output_weight_gradient, gain_columns), '...  119 us
    dot_general x1, matrix products, on_device(): upper = jnp.dot(flat, up_weight[0], preferred_element_type=jnp.float32)  35.7 us
    sub x1, other arithmetic, on_device(): weights = jnp.exp(scores - top)  34.3 us
    convert_element_type x2, other arithmetic, on_device(): score_gradient = (probs * (prob_gradient - inner)).astype(jnp.bfloat16)  28.8 us
    all_to_all x1, blocking collectives, on_device(): lax.all_to_all(outgoing, 'expert', split_axis=0, concat_axis=0, tiled=True)  26.6 us
    all_to_all x1, blocking collectives, on_device(): lax.all_to_all(gradient_outgoing, 'expert', split_axis=0, concat_axis=0,...  24.7 us
    dot_general x2, matrix products, on_device(): jnp.einsum('sqhd,skhd->shqk', incoming, values[:, :upto], preferred_eleme...  23.5 us
  transfers between devices with their start and end apart: 6, of which 4 were waited for; matrix products, arithmetic and copies ran while one was open for 6% of the time, Pallas kernels for 0%

profile of v1, /device:TPU:0, one launch (start us, length us, event | category | flops | bytes accessed | tf_op | source)
XLA Modules:
  0.0 984.3 jit_solution(482732953064682736)
XLA Ops:
  43.2 13.4 %fusion.85 = f32[12,512,1024]{2,1,0:T(8,128)} fusion(bf16[1024,12,64]{0,2,1:T(8,128)(2,1)} %bitcast.177, bf16[1,1024,12,64]{1,3,2,0:T(8,128)(2,1)} %bitcast.181), kind=kOutput, calls=%fused_computation.133 | convolution fusion | flops 805306368 | bytes 27525120 | tf_op jit(solution)/shard_map/sqhd,skhd->shqk/dot_general | solution.py:25
  56.6 11.1 %fusion.121 = (f32[12,512]{1,0:T(8,128)}, f32[12,512,512]{1,2,0:T(8,128)}) fusion(pred[512,512]{0,1:T(8,128)(4,1)} %fusion.79, bf16[1,1024,12,64]{1,3,2,0:T(8,128)(2,1)} %bitcast.182, bf16[1,1024,12,64]{1,3,2,0:T(8,128)(2,1)} %bitcast.178), kind=kOutput, calls=%fused_computation.196 | convolution fusion | flops 415236608 | bytes 14442496 | tf_op jit(solution)/shard_map/sub | solution.py:79
  67.6 34.3 %fusion.120 = (f32[12,512]{1,0:T(8,128)}, f32[12,512,1024]{2,1,0:T(8,128)}) fusion(f32[12,512,1024]{2,1,0:T(8,128)} %fusion.85, pred[512,1024]{1,0:T(8,128)(4,1)} %fusion.49), kind=kOutput, calls=%fused_computation.195 | output fusion | flops 37749760 | bytes 50880512 | tf_op jit(solution)/shard_map/sub | solution.py:79
  108.0 10.3 %fusion.71 = bf16[1,512,12,64]{1,3,2,0:T(8,128)(2,1)S(1)} fusion(bf16[1024,12,64]{0,2,1:T(8,128)(2,1)S(1)} %bitcast.195, f32[12,512,1024]{2,1,0:T(8,128)} %get-tuple-element.123, f32[12,512]{1,0:T(8,128)S(1)} %copy-done.50), kind=kOutput, calls=%fused_computation.114 | convolution fusion | flops 818282496 | bytes 27549696 | tf_op jit(solution)/shard_map/shqk,skhd->sqhd/dot_general | solution.py:83
  139.1 26.6 %all_to_all.20 = bf16[8,128,768]{2,1,0:T(8,128)(2,1)S(1)} all-to-all(bf16[8,128,768]{2,1,0:T(8,128)(2,1)} %bitcast.188), channel_id=1, replica_groups=mesh['dp'=4,'expert'=8] {'expert'}, dimensions={0} | all-to-all | bytes 3145728 | tf_op jit(solution)/shard_map/all_to_all | solution.py:112
  165.7 35.7 %multiply_convert_fusion.2 = (bf16[1024,3072]{1,0:T(8,128)(2,1)S(1)}, f32[1024,3072]{1,0:T(8,128)}, f32[1024,3072]{1,0:T(8,128)}) fusion(bf16[1024,768]{1,0:T(8,128)(2,1)S(1)} %bitcast.191, bf16[1,768,3072]{2,1,0:T(8,128)(2,1)} %param.37), kind=kOutput, calls=%fused_computation.16 | convolution fusion | flops 5036310528 | bytes 37748736 | tf_op jit(solution)/shard_map/dot_general | solution.py:115
  201.4 10.7 %fusion.57 = bf16[1024,768]{1,0:T(8,128)(2,1)} fusion(bf16[1024,3072]{1,0:T(8,128)(2,1)S(1)} %get-tuple-element.108, bf16[1,3072,768]{2,1,0:T(8,128)(2,1)} %param.38), kind=kOutput, calls=%fused_computation.102 | convolution fusion | flops 4832624640 | bytes 12582912 | tf_op jit(solution)/shard_map/dot_general | solution.py:117
  219.1 18.4 %all-to-all-done.1 = bf16[8,128,768]{2,1,0:T(8,128)(2,1)} async-done(((bf16[8,128,768]{2,1,0:T(8,128)(2,1)}), bf16[8,128,768]{2,1,0:T(8,128)(2,1)}, u32[]{:S(2)}, u32[]{:S(2)}) %all-to-all-start.1) | async-done | bytes 1572896 | tf_op jit(solution)/shard_map/all_to_all | solution.py:120
  237.5 7.2 gather_fusion
  261.3 24.7 %all_to_all.21 = bf16[8,128,768]{2,1,0:T(8,128)(2,1)S(1)} all-to-all(bf16[8,128,768]{2,1,0:T(8,128)(2,1)} %bitcast.187), channel_id=1, replica_groups=mesh['dp'=4,'expert'=8] {'expert'}, dimensions={0} | all-to-all | bytes 3145728 | tf_op jit(solution)/shard_map/all_to_all | solution.py:140
  285.9 16.4 %add_convert_fusion = bf16[1024,3072]{1,0:T(8,128)(2,1)} fusion(f32[1024,3072]{1,0:T(8,128)} %get-tuple-element.109, f32[1024,3072]{1,0:T(8,128)} %get-tuple-element.129, bf16[1024,768]{1,0:T(8,128)(2,1)S(1)} %bitcast.199, bf16[1,3072,768]{2,1,0:T(8,128)(2,1)} %param.38), kind=kOutput, calls=%fused_computation.15 | convolution fusion | flops 4875878400 | bytes 37748736 | tf_op jit(solution)/shard_map/rd,fd->rf/dot_general | solution.py:157
  302.3 9.5 fusion.54
  316.3 21.0 %all-to-all-done.3 = bf16[8,128,768]{2,1,0:T(8,128)(2,1)} async-done(((bf16[8,128,768]{2,1,0:T(8,128)(2,1)}), bf16[8,128,768]{2,1,0:T(8,128)(2,1)}, u32[]{:S(2)}, u32[]{:S(2)}) %all-to-all-start.3) | async-done | bytes 1572896 | tf_op jit(solution)/shard_map/all_to_all | solution.py:173
  385.8 17.8 %multiply_reduce_fusion = (f32[12,512]{1,0:T(8,128)}, f32[12,512,1024]{2,1,0:T(8,128)}) fusion(f32[12,512,1024]{2,1,0:T(8,128)} %get-tuple-element.123, f32[12,512]{1,0:T(8,128)} %get-tuple-element.122, bf16[1024,12,64]{0,2,1:T(8,128)(2,1)} %bitcast.194, bf16[1,1024,12,64]{1,3,2,0:T(8,128)(2,1)} %bitcast.215), kind=kOutput, calls=%fused_computation.7 | convolution fusion | flops 824174592 | bytes 52748288 | tf_op jit(solution)/shard_map/sqhd,skhd->shqk/dot_general | solution.py:205
  403.6 10.6 %fusion.42 = bf16[1,1024,12,64]{1,3,2,0:T(8,128)(2,1)S(1)} fusion(f32[1,512,12,64]{1,3,2,0:T(8,128)} %fusion.60, bf16[1,1024,12,64]{1,3,2,0:T(8,128)(2,1)} %bitcast.216, f32[12,512,1024]{2,1,0:T(8,128)} %get-tuple-element.123, f32[12,512]{1,0:T(8,128)} %get-tuple-element.122), kind=kOutput, calls=%fused_computation.81 | convolution fusion | flops 819462144 | bytes 29130752 | tf_op jit(solution)/shard_map/shqk,sqhd->skhd/dot_general | solution.py:226
  414.3 21.8 %multiply_convert_fusion = bf16[12,512,1024]{2,1,0:T(8,128)(2,1)} fusion(f32[12,512,1024]{2,1,0:T(8,128)} %get-tuple-element.133, f32[12,512]{1,0:T(8,128)S(1)} %copy-done.52, f32[12,512,1024]{2,1,0:T(8,128)} %get-tuple-element.123, f32[12,512]{1,0:T(8,128)S(1)} %copy-done.51), kind=kLoop, calls=%fused_computation.6 | loop fusion | flops 25165824 | bytes 62963712 | tf_op jit(solution)/shard_map/convert_element_type | solution.py:209
  436.1 8.6 fusion.77
  461.4 9.1 convolution_convert_fusion.1
  470.6 9.4 convolution_convert_fusion.2
  480.1 119.1 %all-reduce.7.cloned.1.call-done = (f32[768,2304]{1,0:T(8,128)}, f32[768,768]{1,0:T(8,128)}) async-done(((f32[768,2304]{1,0:T(8,128)}, f32[768,768]{1,0:T(8,128)}), (f32[768,2304]{1,0:T(8,128)}, f32[768,768]{1,0:T(8,128)})) %all-reduce.7.cloned.1.call-update) | async-done | bytes 9437200 | tf_op jit(solution)/shard_map/psum | solution.py:250
  603.6 7.9 fusion.123
  627.6 23.4 %psum.46 = f32[768,4]{0,1:T(4,128)} all-reduce(f32[768,4]{0,1:T(4,128)S(1)} %pad_maximum_fusion.5), channel_id=1, replica_groups=mesh['dp'=4,'expert'=8] {'expert'}, use_global_device_ids=true, to_apply=%region_29.31 | all-reduce | flops 3072 | bytes 24576 | tf_op jit(solution)/shard_map/psum | solution.py:250
  651.0 20.8 %psum.47 = f32[768,4]{0,1:T(4,128)S(1)} all-reduce(f32[768,4]{0,1:T(4,128)} %psum.46), channel_id=1, replica_groups=mesh['dp'=4,'expert'=8] {'dp'}, use_global_device_ids=true, to_apply=%region_30.32 | all-reduce | flops 3072 | bytes 24576 | tf_op jit(solution)/shard_map/psum | solution.py:249
  678.3 293.6 %all-reduce.9.cloned.1.call-done = (f32[768,2304]{1,0:T(8,128)}, f32[768,768]{1,0:T(8,128)}) async-done(((f32[768,2304]{1,0:T(8,128)}, f32[768,768]{1,0:T(8,128)}), (f32[768,2304]{1,0:T(8,128)}, f32[768,768]{1,0:T(8,128)})) %all-reduce.9.cloned.1.call-update) | async-done | bytes 9437200 | tf_op jit(solution)/shard_map/psum | solution.py:249
  (241 shorter events, 185.5 us)
Async XLA Ops:
  8.0 19.3 %copy-start = (bf16[768,2304]{1,0:T(8,128)(2,1)S(1)}, bf16[768,2304]{1,0:T(8,128)(2,1)}, u32[]{:S(2)}) copy-start(bf16[768,2304]{1,0:T(8,128)(2,1)} %param.31) | copy-start | bytes 10616836
  9.9 108.6 %copy-start.56 = (f32[1024]{0:T(1024)}, f32[1024]{0:T(1024)S(1)}, u32[]{:S(2)}) copy-start(f32[1024]{0:T(1024)S(1)} %fusion.106) | copy-start | bytes 12292
  24.8 6.9 copy-start.30
  132.0 69.4 %copy-start.58 = (s32[1024]{0:T(1024)}, s32[1024]{0:T(1024)S(1)}, u32[]{:S(2)}) copy-start(s32[1024]{0:T(1024)S(1)} %get-tuple-element.107) | copy-start | bytes 12292
  165.7 35.7 %copy-start.21 = (bf16[8,128,768]{2,1,0:T(8,128)(2,1)}, bf16[8,128,768]{2,1,0:T(8,128)(2,1)S(1)}, u32[]{:S(2)}) copy-start(bf16[8,128,768]{2,1,0:T(8,128)(2,1)S(1)} %all_to_all.20) | copy-start | bytes 4718596
  201.4 10.7 %copy-start.72 = (bf16[1024,3072]{1,0:T(8,128)(2,1)}, bf16[1024,3072]{1,0:T(8,128)(2,1)S(1)}, u32[]{:S(2)}) copy-start(bf16[1024,3072]{1,0:T(8,128)(2,1)S(1)} %get-tuple-element.108) | copy-start | bytes 18874372
  212.1 6.9 copy-start.59
  212.1 6.9 copy-start.45
  212.1 25.4 %all-to-all-start.1 = ((bf16[8,128,768]{2,1,0:T(8,128)(2,1)}), bf16[8,128,768]{2,1,0:T(8,128)(2,1)}, u32[]{:S(2)}, u32[]{:S(2)}) async-start(bf16[8,128,768]{2,1,0:T(8,128)(2,1)} %bitcast.204), calls=%async_computation.1 | async-start | bytes 3145728 | tf_op jit(solution)/shard_map/all_to_all | solution.py:120
  219.1 28.2 %copy-start.48 = (f32[1024]{0:T(1024)}, f32[1024]{0:T(1024)S(1)}, u32[]{:S(2)}) copy-start(f32[1024]{0:T(1024)S(1)} %broadcast_select_fusion.1) | copy-start | bytes 12292
  285.9 16.4 %copy-start.26 = (bf16[8,128,768]{2,1,0:T(8,128)(2,1)}, bf16[8,128,768]{2,1,0:T(8,128)(2,1)S(1)}, u32[]{:S(2)}) copy-start(bf16[8,128,768]{2,1,0:T(8,128)(2,1)S(1)} %all_to_all.21) | copy-start | bytes 4718596
  311.8 25.5 %all-to-all-start.3 = ((bf16[8,128,768]{2,1,0:T(8,128)(2,1)}), bf16[8,128,768]{2,1,0:T(8,128)(2,1)}, u32[]{:S(2)}, u32[]{:S(2)}) async-start(bf16[8,128,768]{2,1,0:T(8,128)(2,1)} %bitcast.203), calls=%async_computation.3 | async-start | bytes 3145728 | tf_op jit(solution)/shard_map/all_to_all | solution.py:173
  316.2 283.0 %all-reduce.7.cloned.1.call-start = ((), (), s32[]{:S(2)}) async-start(), calls=%async_computation.8 | async-start | bytes 18874368 | tf_op jit(solution)/shard_map/psum | solution.py:250
  373.7 6.9 copy-start.8
  403.6 10.6 %copy-start.51 = (f32[12,512]{1,0:T(8,128)S(1)}, f32[12,512]{1,0:T(8,128)}, u32[]{:S(2)}) copy-start(f32[12,512]{1,0:T(8,128)} %get-tuple-element.122) | copy-start | bytes 73732
  403.6 10.6 %copy-start.52 = (f32[12,512]{1,0:T(8,128)S(1)}, f32[12,512]{1,0:T(8,128)}, u32[]{:S(2)}) copy-start(f32[12,512]{1,0:T(8,128)} %get-tuple-element.132) | copy-start | bytes 73732
  414.2 37.8 %copy-start.70 = (bf16[1,1024,12,64]{1,3,2,0:T(8,128)(2,1)}, bf16[1,1024,12,64]{1,3,2,0:T(8,128)(2,1)S(1)}, u32[]{:S(2)}) copy-start(bf16[1,1024,12,64]{1,3,2,0:T(8,128)(2,1)S(1)} %fusion.42) | copy-start | bytes 4718596
  414.2 21.9 %copy-start.9 = (bf16[1024,768]{0,1:T(8,128)(2,1)S(1)}, bf16[1024,768]{0,1:T(8,128)(2,1)}, u32[]{:S(2)}) copy-start(bf16[1024,768]{0,1:T(8,128)(2,1)} %copy.46) | copy-start | bytes 4718596
  436.1 8.7 copy-start.16
  436.1 8.7 copy-start.18
  444.8 7.0 copy-start.20
  461.4 211.0 %reduce-scatter.5.cloned.1.call-start = ((), (), s32[]{:S(2)}) async-start(), calls=%async_computation.7 | async-start | bytes 5898240 | tf_op jit(solution)/shard_map/reduce_scatter | solution.py:149
  470.6 204.7 %reduce-scatter.3.cloned.1.call-start = ((), (), s32[]{:S(2)}) async-start(), calls=%async_computation.6 | async-start | bytes 5898240 | tf_op jit(solution)/shard_map/reduce_scatter | solution.py:162
  480.1 491.8 %all-reduce.9.cloned.1.call-start = ((), (), s32[]{:S(2)}) async-start(), calls=%async_computation.9 | async-start | bytes 18874368 | tf_op jit(solution)/shard_map/psum | solution.py:249
  (58 other events, 201.2 us)
Sparse Core Ops, SparseCore 0:
  461.5 137.6 all-reduce.6
Sparse Core Ops, SparseCore 1:
  470.7 84.5 reduce-scatter.4
  557.4 85.6 reduce-scatter.2
  645.8 326.0 all-reduce.8
